TPU v7x, 32 devices: a whole 2x2x4 slice. The times are simulated.
32 devices in a mesh: row: 4 (over z), col: 8 (over y, x, core).
Axes of the slice: x: 2, y: 2, z: 4, core: 2. Of those that a mesh axis runs over, the one named last changes fastest.
Arguments:
- species: float32 [53, 32, 64, 256], P(None, 'row', 'col'), may hold values from 0.05 to 2
- velocity: float32 [3, 32, 64, 256], P(None, 'row', 'col'), may hold values from -1 to 1
- diffusivity: float32 [53], replicated, may hold values from 0.02 to 0.1
- divergence: float32 [32, 64, 256], P('row', 'col'), may hold values from -6 to 6
- log_rates: float32 [325], replicated, may hold values from -3 to 1
- reactants: int32 [325, 53], replicated, may hold values from 0 to 3, as said below
- products: int32 [325, 53], replicated, may hold values from 0 to 3, as said below
- heat_weights: float32 [53], replicated, may hold values from -0.875 to 0.875
- substeps: int32 [32, 64, 2], P('row', 'col'), may hold values from 1 to 6
Outputs:
- reacted: float32 [53, 32, 64, 256], P(None, 'row', 'col')
- pressure: float32 [32, 64, 256], P('row', 'col')
Inputs may be any that keep to these rules, and one draw needn't show every extreme that they name: `reactants`: each reaction has one or two reactant species. `products`: each reaction has one or two product species.
All inputs are finite; a program needn't handle non-finite values.
Results may differ from a plain program's by a relative error of at most 0.0003.
Values sent between devices are 32-bit elements; how exact they have to be, the bound alone decides.
No kernel may reach another device: no remote copies, remote signals or barrier semaphores. Data moves between devices by JAX's collectives and lax.ppermute only.
A program may use at most 128 MiB of HBM per device.

v0:
```python
import math
import jax
import jax.numpy as jnp
from jax import lax
from jax.sharding import PartitionSpec as P

BLOCK = 128
MAXSUB = 6
time_step = 0.2
screen = 0.004
highest = lax.Precision.HIGHEST
group_blocks = 8


def with_halo(block, sides, width):
    for axis, dim in sides:
        count = lax.axis_size(axis)
        forward = [(i, i + 1) for i in range(count - 1)]
        backward = [(target, source) for source, target in forward]
        low = lax.ppermute(
            lax.slice_in_dim(block, block.shape[dim] - width, None, axis=dim), axis, forward
        )
        high = lax.ppermute(lax.slice_in_dim(block, 0, width, axis=dim), axis, backward)
        block = jnp.concatenate([low, block, high], axis=dim)
    return block


def cosine_table(length):
    wave = jnp.arange(length, dtype=jnp.float32)
    sample = jnp.arange(length, dtype=jnp.float32) + 0.5
    weight = jnp.where(wave == 0, jnp.sqrt(1.0 / length), jnp.sqrt(2.0 / length)).astype(
        jnp.float32
    )
    return weight[:, None] * jnp.cos(jnp.pi * wave[:, None] * sample[None, :] / length)


def mode_values(length):
    wave = jnp.arange(length, dtype=jnp.float32)
    return 2.0 - 2.0 * jnp.cos(jnp.pi * wave / length)


def transport(centre, padded, velocity, diffusivity):
    x_minus = padded[:, :-2, 1:-1, 1:-1]
    x_plus = padded[:, 2:, 1:-1, 1:-1]
    y_minus = padded[:, 1:-1, :-2, 1:-1]
    y_plus = padded[:, 1:-1, 2:, 1:-1]
    z_minus = padded[:, 1:-1, 1:-1, :-2]
    z_plus = padded[:, 1:-1, 1:-1, 2:]
    lateral = x_minus + x_plus + (y_minus + y_plus) + (z_minus + z_plus) - 6.0 * centre
    upwind = jnp.maximum(velocity, 0.0)[:, None]
    downwind = jnp.minimum(velocity, 0.0)[:, None]
    carried = upwind[0] * (centre - x_minus) + downwind[0] * (x_plus - centre)
    carried = carried + upwind[1] * (centre - y_minus) + downwind[1] * (y_plus - centre)
    carried = carried + upwind[2] * (centre - z_minus) + downwind[2] * (z_plus - centre)
    return centre + time_step * (diffusivity[:, None, None, None] * lateral - carried)


def clamp_edges(padded, position, last_index, dimension):
    extent = padded.shape[dimension]
    lower = jnp.where(
        position == 0,
        lax.slice_in_dim(padded, 1, 2, axis=dimension),
        lax.slice_in_dim(padded, 0, 1, axis=dimension),
    )
    upper = jnp.where(
        position == last_index,
        lax.slice_in_dim(padded, extent - 2, extent - 1, axis=dimension),
        lax.slice_in_dim(padded, extent - 1, extent, axis=dimension),
    )
    return jnp.concatenate(
        [lower, lax.slice_in_dim(padded, 1, extent - 1, axis=dimension), upper], axis=dimension
    )


def react_step(conc, step_size, log_rates, react_float, prod_float):
    rates = jnp.exp(
        log_rates[:, None]
        + jnp.dot(react_float, jnp.log(conc), precision=highest, preferred_element_type=jnp.float32)
    )
    gained = jnp.dot(prod_float.T, rates, precision=highest, preferred_element_type=jnp.float32)
    lost = jnp.dot(react_float.T, rates, precision=highest, preferred_element_type=jnp.float32)
    return conc * (conc + step_size * gained) / (conc + step_size * lost)


def kinetics(blocks, counts, log_rates, react_float, prod_float):
    species_count = blocks.shape[0]
    block_count = blocks.shape[1]
    block_cells = blocks.shape[2]
    group_size = math.gcd(group_blocks, block_count)
    ordering = jnp.argsort(-counts, stable=True)
    current = jnp.take(blocks, ordering, axis=1)
    ordered_counts = jnp.take(counts, ordering)
    step_sizes = time_step / ordered_counts.astype(jnp.float32)
    for level in range(MAXSUB):
        active_count = jnp.sum((ordered_counts > level).astype(jnp.int32))
        turn_count = (active_count + group_size - 1) // group_size

        def one_turn(turn_index, holding, level=level):
            start_block = turn_index * group_size
            section = lax.dynamic_slice_in_dim(holding, start_block, group_size, 1)
            still_live = (
                lax.dynamic_slice_in_dim(ordered_counts, start_block, group_size, 0) > level
            )
            sizes_here = lax.dynamic_slice_in_dim(step_sizes, start_block, group_size, 0)
            cell_sizes = jnp.broadcast_to(sizes_here[:, None], (group_size, block_cells)).reshape(
                group_size * block_cells
            )
            flat_section = section.reshape(species_count, group_size * block_cells)
            fresh = react_step(
                flat_section, cell_sizes[None, :], log_rates, react_float, prod_float
            )
            fresh = fresh.reshape(section.shape)
            updated = jnp.where(still_live[None, :, None], fresh, section)
            return lax.dynamic_update_slice_in_dim(holding, updated, start_block, 1)

        current = lax.fori_loop(0, turn_count, one_turn, current)
    return jnp.take(current, jnp.argsort(ordering), axis=1)


def local(
    species,
    velocity,
    diffusivity,
    divergence,
    log_rates,
    reactants,
    products,
    heat_weights,
    substeps,
):
    species_count, cells_x, cells_y, cells_z = species.shape
    rows_count = lax.axis_size("row")
    cols_count = lax.axis_size("col")
    device_count = rows_count * cols_count
    padded = with_halo(species, (("row", 1), ("col", 2)), 1)
    padded = clamp_edges(padded, lax.axis_index("row"), rows_count - 1, 1)
    padded = clamp_edges(padded, lax.axis_index("col"), cols_count - 1, 2)
    padded = jnp.pad(padded, ((0, 0), (0, 0), (0, 0), (1, 1)), mode="edge")
    moved = transport(species, padded, velocity, diffusivity)
    react_float = reactants.astype(jnp.float32)
    prod_float = products.astype(jnp.float32)
    block_count = substeps.shape[0] * substeps.shape[1] * substeps.shape[2]
    blocks = moved.reshape(species_count, block_count, BLOCK)
    counts = substeps.reshape(block_count)
    reacted = kinetics(blocks, counts, log_rates, react_float, prod_float).reshape(
        species_count, cells_x, cells_y, cells_z
    )
    heat = jnp.einsum("s,sxyz->xyz", heat_weights, reacted - moved, precision=highest) / time_step
    source = divergence - heat
    table_z = cosine_table(cells_z)
    forward = jnp.einsum("kz,xyz->kxy", table_z, source, precision=highest).reshape(
        cells_z, cells_x * cells_y
    )
    planes = lax.all_to_all(forward, ("row", "col"), split_axis=0, concat_axis=1, tiled=True)
    depth = cells_z // device_count
    planes = planes.reshape(depth, rows_count, cols_count, cells_x, cells_y)
    table_x = cosine_table(rows_count * cells_x).reshape(rows_count * cells_x, rows_count, cells_x)
    table_y = cosine_table(cols_count * cells_y).reshape(cols_count * cells_y, cols_count, cells_y)
    spectrum = jnp.einsum("ari,zrcij->zacj", table_x, planes, precision=highest)
    spectrum = jnp.einsum("bcj,zacj->zab", table_y, spectrum, precision=highest)
    device_index = lax.axis_index("row") * cols_count + lax.axis_index("col")
    z_values = lax.dynamic_slice_in_dim(mode_values(cells_z), device_index * depth, depth, 0)
    denominator = (
        screen
        + z_values[:, None, None]
        + mode_values(rows_count * cells_x)[None, :, None]
        + mode_values(cols_count * cells_y)[None, None, :]
    )
    spectrum = spectrum / denominator
    spectrum = jnp.einsum("bcj,zab->zacj", table_y, spectrum, precision=highest)
    spectrum = jnp.einsum("ari,zacj->zrcij", table_x, spectrum, precision=highest)
    outgoing = spectrum.reshape(depth, device_count * cells_x * cells_y)
    columns = lax.all_to_all(outgoing, ("row", "col"), split_axis=1, concat_axis=0, tiled=True)
    columns = columns.reshape(cells_z, cells_x, cells_y)
    pressure = jnp.einsum("kz,kxy->xyz", table_z, columns, precision=highest)
    return (reacted, pressure)


def solution(mesh):
    return jax.shard_map(
        local,
        mesh=mesh,
        in_specs=(
            P(None, "row", "col", None),
            P(None, "row", "col", None),
            P(),
            P("row", "col", None),
            P(),
            P(),
            P(),
            P(),
            P("row", "col", None),
        ),
        out_specs=(P(None, "row", "col", None), P("row", "col", None)),
        check_vma=False,
    )
```

profile of v0, /device:TPU:0, one launch (start us, length us, event | category | flops | bytes accessed | tf_op | source)
XLA Modules:
  0.0 622.2 jit_solution(320372246341972101)
XLA Ops:
  1.9 5.0 collective-permute-start
  28.7 3.8 collective-permute-done.3
  36.0 4.0 pad_maximum_fusion.1
  40.0 4.0 slice.143
  45.5 4.2 pad_maximum_fusion.2
  49.7 8.3 %fusion.110 = (f32[53,10,10,1]{3,2,1,0:T(8,128)}, f32[53,10,10,1]{3,2,1,0:T(8,128)}) fusion(f32[53,10,10,256]{3,2,1,0:T(8,128)} %pad_maximum_fusion.2), kind=kLoop, calls=%fused_computation.221 | loop fusion | bytes 84800 | tf_op jit(solution)/shard_map/jit(_pad)/slice | solution.py:138
  58.0 12.7 %multiply_add_fusion = f32[53,8,8,256]{3,2,1,0:T(8,128)} fusion(f32[53,8,8,256]{3,2,1,0:T(8,128)S(1)} %copy-done.2, f32[53,10,1,256]{3,2,1,0:T(1,128)S(1)} %get-tuple-element.411, f32[53,10,8,256]{3,2,1,0:T(8,128)S(1)} %slice.143, f32[53,10,1,256]{3,2,1,0:T(1,128)S(1)} %get-tuple-element.410, f32[53,10,10,1]{3,2,1,0:T(8,128)} %get-tuple-element.409, ...), kind=kLoop, calls=%fused_computation.116 | loop fusion | flops 32997376 | bytes 18237044 | tf_op jit(solution)/shard_map/add | solution.py:55
  70.7 4.5 reshape.242
  75.2 5.8 copy.42
  81.0 4.7 gather_fusion.1
  90.4 105.9 %while.60 = (s32[]{:T(128)}, f32[53,128,128]{2,1,0:T(8,128)}, s32[]{:T(128)}, s32[128]{0:T(128)S(1)}, f32[128]{0:T(128)S(1)}, /*index=5*/f32[325]{0:T(512)S(1)},...) while((s32[]{:T(128)}, f32[53,128,128]{2,1,0:T(8,128)}, ...), condition=%wide.region_3.5_spmd, body=%wide.region_2.4_spmd.sunk | while | flops 635695104 | bytes 7966159 | solution.py:116
  196.4 66.1 %while.61 = (s32[]{:T(128)}, f32[53,128,128]{2,1,0:T(8,128)}, s32[]{:T(128)}, s32[128]{0:T(128)S(1)}, f32[128]{0:T(128)S(1)}, /*index=5*/f32[325]{0:T(512)S(1)},...) while((s32[]{:T(128)}, f32[53,128,128]{2,1,0:T(8,128)}, ...), condition=%wide.region_6.8_spmd, body=%wide.region_5.7_spmd.sunk | while | flops 635695104 | bytes 7966159 | solution.py:116
  262.5 26.4 %while.62 = (s32[]{:T(128)}, f32[53,128,128]{2,1,0:T(8,128)}, s32[]{:T(128)}, s32[128]{0:T(128)S(1)}, f32[128]{0:T(128)S(1)}, /*index=5*/f32[325]{0:T(512)S(1)},...) while((s32[]{:T(128)}, f32[53,128,128]{2,1,0:T(8,128)}, ...), condition=%wide.region_9.11_spmd, body=%wide.region_8.10_spmd.sunk | while | flops 635695104 | bytes 7966159 | solution.py:116
  288.9 26.4 %while.63 = (s32[]{:T(128)}, f32[53,128,128]{2,1,0:T(8,128)}, s32[]{:T(128)}, s32[128]{0:T(128)S(1)}, f32[128]{0:T(128)S(1)}, /*index=5*/f32[325]{0:T(512)S(1)},...) while((s32[]{:T(128)}, f32[53,128,128]{2,1,0:T(8,128)}, ...), condition=%wide.region_12.14_spmd, body=%wide.region_11.13_spmd.sunk | while | flops 635695104 | bytes 7966159 | solution.py:116
  315.3 20.2 %while.64 = (s32[]{:T(128)}, f32[53,128,128]{2,1,0:T(8,128)}, s32[]{:T(128)}, s32[128]{0:T(128)S(1)}, f32[128]{0:T(128)S(1)}, /*index=5*/f32[325]{0:T(512)S(1)},...) while((s32[]{:T(128)}, f32[53,128,128]{2,1,0:T(8,128)}, ...), condition=%wide.region_15.17_spmd, body=%wide.region_14.16_spmd.sunk | while | flops 635695104 | bytes 7966159 | solution.py:116
  335.6 6.8 %while.65 = (s32[]{:T(128)}, f32[53,128,128]{2,1,0:T(8,128)}, s32[]{:T(128)}, s32[128]{0:T(128)S(1)}, f32[128]{0:T(128)S(1)}, /*index=5*/f32[325]{0:T(512)S(1)},...) while((s32[]{:T(128)}, f32[53,128,128]{2,1,0:T(8,128)}, ...), condition=%wide.region_18.20_spmd, body=%wide.region_17.19_spmd.sunk | while | flops 635695104 | bytes 7966159 | solution.py:116
  342.3 5.8 copy.46
  348.1 4.7 gather_fusion.2
  357.5 5.1 reshape.244
  365.4 4.1 fusion.54
  372.9 221.0 %all-to-all-start = ((f32[32,1,512]{2,1,0:T(1,128)}), f32[32,1,512]{2,1,0:T(1,128)S(1)}, u32[]{:S(2)}, u32[]{:S(2)}) async-start(f32[32,1,512]{2,1,0:T(1,128)} %reshape.290), calls=%async_computation | async-start | bytes 131072 | tf_op jit(solution)/shard_map/all_to_all | solution.py:154
  593.9 7.4 %all-to-all-done = f32[32,1,512]{2,1,0:T(1,128)S(1)} async-done(((f32[32,1,512]{2,1,0:T(1,128)}), f32[32,1,512]{2,1,0:T(1,128)S(1)}, u32[]{:S(2)}, u32[]{:S(2)}) %all-to-all-start) | async-done | bytes 65568 | tf_op jit(solution)/shard_map/all_to_all | solution.py:154
  608.3 9.1 %all_to_all.32 = f32[32,1,512]{2,1,0:T(1,128)S(1)} all-to-all(f32[32,1,512]{2,1,0:T(1,128)S(1)} %reshape.292), channel_id=1, replica_groups=mesh['row'=4,'col'=8] {'row','col'}, dimensions={0} | all-to-all | bytes 131072 | tf_op jit(solution)/shard_map/all_to_all | solution.py:173
  618.6 3.3 fusion.58
  (502 shorter events, 296.7 us)
Async XLA Ops:
  0.6 364.7 %copy-start = (f32[53]{0:T(128)S(1)}, f32[53]{0:T(128)}, u32[]{:S(2)}) copy-start(f32[53]{0:T(128)} %param.30) | copy-start | bytes 640
  1.9 20.8 %collective-permute-start = (f32[53,1,8,256]{3,2,1,0:T(8,128)S(1)}, f32[53,1,8,256]{3,2,1,0:T(8,128)S(1)}, u32[]{:S(2)}, u32[]{:S(2)}) collective-permute-start(f32[53,1,8,256]{3,2,1,0:T(8,128)S(1)} %get-tuple-element.417), channel_id=1, source_target_pairs={{0,8},{8,16},{16,24},{1,9},{9,17},{17,25},{2,10},{10,18},{18,26},{... | collective-permute-start | bytes 1302536 | tf_op jit(solution)/shard_map/ppermute | solution.py:20
  6.8 18.1 %collective-permute-start.1 = (f32[53,1,8,256]{3,2,1,0:T(8,128)S(1)}, f32[53,1,8,256]{3,2,1,0:T(8,128)S(1)}, u32[]{:S(2)}, u32[]{:S(2)}) collective-permute-start(f32[53,1,8,256]{3,2,1,0:T(8,128)S(1)} %get-tuple-element.416), channel_id=1, source_target_pairs={{8,0},{16,8},{24,16},{9,1},{17,9},{25,17},{10,2},{18,10},{26,18},{... | collective-permute-start | bytes 1302536 | tf_op jit(solution)/shard_map/ppermute | solution.py:23
  22.7 5.9 copy-start.4
  25.7 3.0 collective-permute-start.2
  27.2 5.4 collective-permute-start.3
  49.7 8.3 %copy-start.2 = (f32[53,8,8,256]{3,2,1,0:T(8,128)S(1)}, f32[53,8,8,256]{3,2,1,0:T(8,128)}, u32[]{:S(2)}) copy-start(f32[53,8,8,256]{3,2,1,0:T(8,128)} %param.23) | copy-start | bytes 10420228
  49.7 8.3 %copy-start.5 = (f32[53]{0:T(128)S(1)}, f32[53]{0:T(128)}, u32[]{:S(2)}) copy-start(f32[53]{0:T(128)} %param.25) | copy-start | bytes 640
  88.0 2.4 copy-start.3
  357.5 5.1 copy-start.1
  365.3 4.1 copy-start.6
  372.9 228.5 %all-to-all-start = ((f32[32,1,512]{2,1,0:T(1,128)}), f32[32,1,512]{2,1,0:T(1,128)S(1)}, u32[]{:S(2)}, u32[]{:S(2)}) async-start(f32[32,1,512]{2,1,0:T(1,128)} %reshape.290), calls=%async_computation | async-start | bytes 131072 | tf_op jit(solution)/shard_map/all_to_all | solution.py:154
where the time goes:
time: 630 us; the launch traced here: 622 us
  starting transfers between devices  230 us (37%)
  matrix products  149 us (24%)
  other arithmetic  108 us (17%)
  local copies, waits for them, and re-layouts  107 us (17%)
  waiting for transfers between devices  11.3 us (2%)
  blocking collectives  9.1 us (1%)
    all_to_all x1, starting transfers between devices, local(): lax.all_to_all(forward, ('row', 'col'), split_axis=0, concat_axis=1, tile...  221 us
    dynamic_update_slice x38, other arithmetic, one_turn(): return lax.dynamic_update_slice_in_dim(holding, updated, start_block, 1)  64.9 us
    dot_general x38, matrix products, react_step(): jnp.dot(react_float, jnp.log(conc), precision=highest, preferred_element_...  49.1 us
    dot_general x38, matrix products, react_step(): jnp.dot(prod_float.T, rates, precision=highest, preferred_element_type=jn...  43.7 us
    dot_general x38, matrix products, react_step(): jnp.dot(react_float.T, rates, precision=highest, preferred_element_type=j...  42.6 us
    dynamic_slice x38, local copies, waits for them, and re-layouts, one_turn(): section = lax.dynamic_slice_in_dim(holding, start_block, group_size, 1)  36.1 us
    add x1, other arithmetic, transport(): centre + time_step * (diffusivity[:, None, None, None] * lateral - carried)  12.7 us
  transfers between devices with their start and end apart: 5, of which 3 were waited for; matrix products, arithmetic and copies ran while one was open for 2% of the time, Pallas kernels for 0%

commit v1 on v0

--- a/solution.py
+++ b/solution.py
@@ -151,7 +151,10 @@
     forward = jnp.einsum("kz,xyz->kxy", table_z, source, precision=highest).reshape(
         cells_z, cells_x * cells_y
     )
-    planes = lax.all_to_all(forward, ("row", "col"), split_axis=0, concat_axis=1, tiled=True)
+    count_2 = lax.axis_size(("row", "col"))
+    pieces = jnp.stack(jnp.split(forward, count_2, axis=0), axis=0)
+    pieces = lax.all_to_all(pieces, ("row", "col"), split_axis=0, concat_axis=0)
+    planes = jnp.concatenate(pieces, axis=1)
     depth = cells_z // device_count
     planes = planes.reshape(depth, rows_count, cols_count, cells_x, cells_y)
     table_x = cosine_table(rows_count * cells_x).reshape(rows_count * cells_x, rows_count, cells_x)

time: 630 us -> 629 us (level)
  transfers between devices with their start and end apart: 5 -> 5, of which waited for: 3 -> 2; matrix products, arithmetic and copies ran while one was open for 2% -> 3% of each run, Pallas kernels for 0% -> 0%
where the time goes in v1:
time: 629 us; the launch traced here: 622 us
  starting transfers between devices  230 us (37%)
  matrix products  149 us (24%)
  other arithmetic  112 us (18%)
  local copies, waits for them, and re-layouts  104 us (17%)
  waiting for transfers between devices  9.93 us (2%)
  blocking collectives  9.1 us (1%)
    all_to_all x1, starting transfers between devices, local(): pieces = lax.all_to_all(pieces, ('row', 'col'), split_axis=0, concat_axis=0)  221 us
    dynamic_update_slice x38, other arithmetic, one_turn(): return lax.dynamic_update_slice_in_dim(holding, updated, start_block, 1)  64.7 us
    dot_general x38, matrix products, react_step(): jnp.dot(react_float, jnp.log(conc), precision=highest, preferred_element_...  49.2 us
    dot_general x38, matrix products, react_step(): jnp.dot(prod_float.T, rates, precision=highest, preferred_element_type=jn...  43.7 us
    dot_general x38, matrix products, react_step(): jnp.dot(react_float.T, rates, precision=highest, preferred_element_type=j...  42.9 us
    dynamic_slice x38, local copies, waits for them, and re-layouts, one_turn(): section = lax.dynamic_slice_in_dim(holding, start_block, group_size, 1)  36.1 us
    add x1, other arithmetic, transport(): centre + time_step * (diffusivity[:, None, None, None] * lateral - carried)  15.6 us
  transfers between devices with their start and end apart: 5, of which 2 were waited for; matrix products, arithmetic and copies ran while one was open for 3% of the time, Pallas kernels for 0%

profile of v1, /device:TPU:0, one launch (start us, length us, event | category | flops | bytes accessed | tf_op | source)
XLA Modules:
  0.0 621.8 jit_solution(8798487617708987384)
XLA Ops:
  1.9 5.0 collective-permute-start
  9.1 2.5 sort.34
  11.7 2.5 sort.35
  34.0 2.5 collective-permute-done.3
  46.6 5.0 fusion.110
  51.6 15.6 %multiply_add_fusion = f32[53,8,8,256]{3,2,1,0:T(8,128)} fusion(f32[53,8,8,256]{3,2,1,0:T(8,128)} %param.23, f32[53,10,1,256]{3,2,1,0:T(1,128)} %copy-done.1, f32[53,10,8,256]{3,2,1,0:T(8,128)S(1)} %slice.175, f32[53,10,1,256]{3,2,1,0:T(1,128)S(1)} %get-tuple-element.410, f32[53,10,10,1]{3,2,1,0:T(8,128)} %get-tuple-element.409, ...), kind=kLoop, calls=%fused_computation.116 | loop fusion | flops 32997376 | bytes 18237044 | tf_op jit(solution)/shard_map/add | solution.py:55
  67.2 4.7 reshape.301
  71.9 5.8 copy.73
  77.7 4.7 gather_fusion.1
  87.3 105.8 %while.60 = (s32[]{:T(128)}, f32[53,128,128]{2,1,0:T(8,128)}, s32[]{:T(128)}, s32[128]{0:T(128)S(1)}, f32[128]{0:T(128)S(1)}, /*index=5*/f32[325]{0:T(512)S(1)},...) while((s32[]{:T(128)}, f32[53,128,128]{2,1,0:T(8,128)}, ...), condition=%wide.region_3.5_spmd, body=%wide.region_2.4_spmd.sunk | while | flops 635695104 | bytes 7966159 | solution.py:116
  193.1 66.1 %while.61 = (s32[]{:T(128)}, f32[53,128,128]{2,1,0:T(8,128)}, s32[]{:T(128)}, s32[128]{0:T(128)S(1)}, f32[128]{0:T(128)S(1)}, /*index=5*/f32[325]{0:T(512)S(1)},...) while((s32[]{:T(128)}, f32[53,128,128]{2,1,0:T(8,128)}, ...), condition=%wide.region_6.8_spmd, body=%wide.region_5.7_spmd.sunk | while | flops 635695104 | bytes 7966159 | solution.py:116
  259.2 26.8 %while.62 = (s32[]{:T(128)}, f32[53,128,128]{2,1,0:T(8,128)}, s32[]{:T(128)}, s32[128]{0:T(128)S(1)}, f32[128]{0:T(128)S(1)}, /*index=5*/f32[325]{0:T(512)S(1)},...) while((s32[]{:T(128)}, f32[53,128,128]{2,1,0:T(8,128)}, ...), condition=%wide.region_9.11_spmd, body=%wide.region_8.10_spmd.sunk | while | flops 635695104 | bytes 7966159 | solution.py:116
  286.1 26.5 %while.63 = (s32[]{:T(128)}, f32[53,128,128]{2,1,0:T(8,128)}, s32[]{:T(128)}, s32[128]{0:T(128)S(1)}, f32[128]{0:T(128)S(1)}, /*index=5*/f32[325]{0:T(512)S(1)},...) while((s32[]{:T(128)}, f32[53,128,128]{2,1,0:T(8,128)}, ...), condition=%wide.region_12.14_spmd, body=%wide.region_11.13_spmd.sunk | while | flops 635695104 | bytes 7966159 | solution.py:116
  312.5 19.8 %while.64 = (s32[]{:T(128)}, f32[53,128,128]{2,1,0:T(8,128)}, s32[]{:T(128)}, s32[128]{0:T(128)S(1)}, f32[128]{0:T(128)S(1)}, /*index=5*/f32[325]{0:T(512)S(1)},...) while((s32[]{:T(128)}, f32[53,128,128]{2,1,0:T(8,128)}, ...), condition=%wide.region_15.17_spmd, body=%wide.region_14.16_spmd.sunk | while | flops 635695104 | bytes 7966159 | solution.py:116
  332.4 6.8 %while.65 = (s32[]{:T(128)}, f32[53,128,128]{2,1,0:T(8,128)}, s32[]{:T(128)}, s32[128]{0:T(128)S(1)}, f32[128]{0:T(128)S(1)}, /*index=5*/f32[325]{0:T(512)S(1)},...) while((s32[]{:T(128)}, f32[53,128,128]{2,1,0:T(8,128)}, ...), condition=%wide.region_18.20_spmd, body=%wide.region_17.19_spmd.sunk | while | flops 635695104 | bytes 7966159 | solution.py:116
  339.1 5.8 copy.77
  345.0 4.7 gather_fusion.2
  354.4 4.9 reshape.303
  359.4 3.6 sub.104
  363.0 4.1 fusion.54
  372.3 221.2 %all-to-all-start = ((f32[32,1,512]{2,1,0:T(1,128)}), f32[32,1,512]{2,1,0:T(1,128)S(1)}, u32[]{:S(2)}, u32[]{:S(2)}) async-start(f32[32,1,512]{2,1,0:T(1,128)} %reshape.349), calls=%async_computation | async-start | bytes 131072 | tf_op jit(solution)/shard_map/all_to_all | solution.py:156
  593.5 7.4 %all-to-all-done = f32[32,1,512]{2,1,0:T(1,128)S(1)} async-done(((f32[32,1,512]{2,1,0:T(1,128)}), f32[32,1,512]{2,1,0:T(1,128)S(1)}, u32[]{:S(2)}, u32[]{:S(2)}) %all-to-all-start) | async-done | bytes 65568 | tf_op jit(solution)/shard_map/all_to_all | solution.py:156
  607.9 9.1 %all_to_all.21 = f32[32,1,512]{2,1,0:T(1,128)S(1)} all-to-all(f32[32,1,512]{2,1,0:T(1,128)S(1)} %reshape.351), channel_id=1, replica_groups=mesh['row'=4,'col'=8] {'row','col'}, dimensions={0} | all-to-all | bytes 131072 | tf_op jit(solution)/shard_map/all_to_all | solution.py:176
  618.2 3.3 fusion.58
  (590 shorter events, 300.8 us)
Async XLA Ops:
  0.6 362.4 %copy-start = (f32[53]{0:T(128)S(1)}, f32[53]{0:T(128)}, u32[]{:S(2)}) copy-start(f32[53]{0:T(128)} %param.30) | copy-start | bytes 640
  1.9 24.7 %collective-permute-start = (f32[53,1,8,256]{3,2,1,0:T(8,128)S(1)}, f32[53,1,8,256]{3,2,1,0:T(8,128)S(1)}, u32[]{:S(2)}, u32[]{:S(2)}) collective-permute-start(f32[53,1,8,256]{3,2,1,0:T(8,128)S(1)} %get-tuple-element.417), channel_id=1, source_target_pairs={{0,8},{8,16},{16,24},{1,9},{9,17},{17,25},{2,10},{10,18},{18,26},{... | collective-permute-start | bytes 1302536 | tf_op jit(solution)/shard_map/ppermute | solution.py:20
  6.8 22.1 %collective-permute-start.1 = (f32[53,1,8,256]{3,2,1,0:T(8,128)S(1)}, f32[53,1,8,256]{3,2,1,0:T(8,128)S(1)}, u32[]{:S(2)}, u32[]{:S(2)}) collective-permute-start(f32[53,1,8,256]{3,2,1,0:T(8,128)S(1)} %get-tuple-element.416), channel_id=1, source_target_pairs={{8,0},{16,8},{24,16},{9,1},{17,9},{25,17},{10,2},{18,10},{26,18},{... | collective-permute-start | bytes 1302536 | tf_op jit(solution)/shard_map/ppermute | solution.py:23
  14.8 9.3 %copy-start.4 = (s32[1024]{0:T(1024)}, s32[1024]{0:T(1024)S(1)}, u32[]{:S(2)}) copy-start(s32[1024]{0:T(1024)S(1)} %get-tuple-element.462) | copy-start | bytes 12292
  16.6 7.5 %copy-start.10 = (s32[128]{0:T(128)}, s32[128]{0:T(128)S(1)}, u32[]{:S(2)}) copy-start(s32[128]{0:T(128)S(1)} %get-tuple-element.967) | copy-start | bytes 1540
  26.7 6.5 %copy-start.3 = (f32[3,8,8,256]{3,2,1,0:T(8,128)S(1)}, f32[3,8,8,256]{3,2,1,0:T(8,128)}, u32[]{:S(2)}) copy-start(f32[3,8,8,256]{3,2,1,0:T(8,128)} %param.24) | copy-start | bytes 589828
  29.7 4.3 collective-permute-start.2
  31.2 5.4 collective-permute-start.3
  44.0 0.8 copy-start.1
  77.7 4.7 copy-start.12
  84.8 2.4 copy-start.2
  84.9 2.4 copy-start.11
  84.9 2.4 copy-start.15
  345.0 4.7 copy-start.16
  363.0 4.2 copy-start.5
  363.0 4.2 copy-start.6
  363.0 4.2 copy-start.13
  363.0 4.2 copy-start.17
  367.2 235.4 %copy-start.8 = (f32[32]{0:T(128)S(1)}, f32[32]{0:T(128)}, u32[]{:S(2)}) copy-start(f32[32]{0:T(128)} %get-tuple-element.465) | copy-start | bytes 388
  367.2 235.4 %copy-start.9 = (f32[32]{0:T(128)S(1)}, f32[32]{0:T(128)}, u32[]{:S(2)}) copy-start(f32[32]{0:T(128)} %get-tuple-element.466) | copy-start | bytes 388
  368.5 235.9 %copy-start.7 = (f32[8,32]{1,0:T(8,128)S(1)}, f32[8,32]{1,0:T(8,128)}, u32[]{:S(2)}) copy-start(f32[8,32]{1,0:T(8,128)} %broadcast_add_fusion) | copy-start | bytes 3076
  368.6 235.9 %copy-start.14 = (f32[64]{0:T(128)S(1)}, f32[64]{0:T(128)}, u32[]{:S(2)}) copy-start(f32[64]{0:T(128)} %get-tuple-element.467) | copy-start | bytes 772
  368.6 235.9 %copy-start.18 = (f32[64]{0:T(128)S(1)}, f32[64]{0:T(128)}, u32[]{:S(2)}) copy-start(f32[64]{0:T(128)} %get-tuple-element.468) | copy-start | bytes 772
  372.3 228.6 %all-to-all-start = ((f32[32,1,512]{2,1,0:T(1,128)}), f32[32,1,512]{2,1,0:T(1,128)S(1)}, u32[]{:S(2)}, u32[]{:S(2)}) async-start(f32[32,1,512]{2,1,0:T(1,128)} %reshape.349), calls=%async_computation | async-start | bytes 131072 | tf_op jit(solution)/shard_map/all_to_all | solution.py:156
